TPU v7x, 32 devices: a whole 2x2x4 slice. The times are simulated.
32 devices in a mesh: section: 2 (over core), fsdp: 4 (over z), dp: 4 (over y, x).
Axes of the slice: x: 2, y: 2, z: 4, core: 2. Of those that a mesh axis runs over, the one named last changes fastest.
Arguments:
- tokens: bfloat16 [1, 16, 128, 1024], P(None, ('fsdp', 'dp')), may hold values from -6 to 6
- segments: int32 [1, 16, 128], P(None, ('fsdp', 'dp')), may hold values from 0 to 3, never falling along the last dimension, each value on 1 to 64 neighbouring positions
- cotangent: float32 [1, 16, 128, 1024], P(None, ('fsdp', 'dp')), may hold values from -6 to 6
- norm_gains: bfloat16 [2, 2, 1024], P('section', None, 'fsdp'), may hold values from 0.5 to 1.5
- proj_weight: bfloat16 [2, 1024, 3072], P('section', 'fsdp'), may hold values from -0.1875 to 0.1875
- rate_weight: bfloat16 [2, 1024, 8], P('section', 'fsdp'), may hold values from -0.1875 to 0.1875
- out_weight: bfloat16 [2, 1024, 1024], P('section', 'fsdp'), may hold values from -0.375 to 0.375
- up_weight: bfloat16 [2, 1024, 5632], P('section', 'fsdp'), may hold values from -0.1875 to 0.1875
- down_weight: bfloat16 [2, 1024, 2816], P('section', 'fsdp'), may hold values from -0.21875 to 0.21875
- conv_kernels: float32 [2, 4, 2048], P('section'), may hold values from -3 to 3
- head_params: float32 [2, 2, 4], P('section'), may hold values from -2.5 to 0.5
- out_gain: float32 [2, 256], P('section'), may hold values from 0.5 to 1.5
Outputs:
- section_output: bfloat16 [2, 1, 16, 128, 1024], P('section', None, ('fsdp', 'dp'))
- input_grad: float32 [2, 1, 16, 128, 1024], P('section', None, ('fsdp', 'dp'))
- gains_grad: float32 [2, 2, 1024], P('section', None, 'fsdp')
- proj_grad: float32 [2, 1024, 3072], P('section', 'fsdp')
- rate_grad: float32 [2, 1024, 8], P('section', 'fsdp')
- out_grad: float32 [2, 1024, 1024], P('section', 'fsdp')
- up_grad: float32 [2, 1024, 5632], P('section', 'fsdp')
- down_grad: float32 [2, 1024, 2816], P('section', 'fsdp')
- kernel_grad: float32 [2, 4, 2048], P('section')
- head_grad: float32 [2, 2, 4], P('section')
- out_gain_grad: float32 [2, 256], P('section')
Inputs may be any that keep to these rules, and one draw needn't show every extreme that they name: `segments`: within each sequence the numbers never fall, every one of 0 .. 3 occurs, and each document holds 1 to 64 positions, one exactly 64.
All inputs are finite; a program needn't handle non-finite values.
Results may differ from a plain program's by a relative error of at most 0.034.
Values may be sent and summed in bfloat16 or wider, within the bound.
A program may use at most 256 MiB of HBM per device.

v0:
```python
from functools import partial
import jax
import jax.numpy as jnp
from jax import lax
from jax.sharding import PartitionSpec as P

SPAN = 64
highest = lax.Precision.HIGHEST
reset_level = -30.0


def passed_along(value, axis, steps):
    count = lax.axis_size(axis)
    leading, last = (max(0, -steps), min(count, count - steps))
    return lax.ppermute(value, axis, [(source, source + steps) for source in range(leading, last)])


def rms_gain(values, gain_vec):
    return values * lax.rsqrt(jnp.mean(values * values, -1, keepdims=True) + 1e-06) * gain_vec


def swiglu(joined):
    half_width = joined.shape[-1] // 2
    return jax.nn.silu(joined[..., :half_width]) * joined[..., half_width:]


def short_conv(raw_input, kernel, segment):
    length = raw_input.shape[1]
    tap_count = kernel.shape[0]
    total = raw_input * kernel[tap_count - 1]
    for offset in range(1, tap_count):
        shifted = jnp.pad(raw_input, ((0, 0), (offset, 0), (0, 0)))[:, :length]
        earlier = jnp.pad(segment, ((0, 0), (offset, 0)), constant_values=-1)[:, :length]
        total = (
            total
            + jnp.where((earlier == segment)[..., None], shifted, 0.0)
            * kernel[tap_count - 1 - offset]
        )
    return jax.nn.silu(total)


def delta_rule(queries, key_rows, value_rows, beta_gate, decays, block_len):
    batch_size, head_count, length, key_dim = queries.shape
    value_dim = value_rows.shape[-1]
    block_count = length // block_len

    def to_blocks(array):
        return array.reshape(array.shape[:2] + (block_count, block_len) + array.shape[3:])

    queries = to_blocks(queries)
    key_rows = to_blocks(key_rows)
    value_rows = to_blocks(value_rows)
    beta_gate = to_blocks(beta_gate)
    levels = jnp.cumsum(to_blocks(decays), axis=-1)
    places = jnp.arange(block_len)
    lower_mask = places[:, None] >= places[None, :]
    strict_mask = places[:, None] > places[None, :]
    spread = jnp.exp(jnp.where(lower_mask, levels[..., :, None] - levels[..., None, :], -1e30))
    beta_keys = key_rows * beta_gate[..., None]
    key_inner = jnp.einsum("bhncd,bhnmd->bhncm", beta_keys, key_rows, precision=highest) * spread
    system = jnp.where(strict_mask, key_inner, 0.0)
    right_side = jnp.concatenate(
        [beta_keys * jnp.exp(levels)[..., None], value_rows * beta_gate[..., None]], -1
    )
    solved = lax.linalg.triangular_solve(
        system, right_side, left_side=True, lower=True, unit_diagonal=True
    )
    solved_keys = solved[..., :key_dim]
    solved_values = solved[..., key_dim:]
    scores = jnp.einsum("bhncd,bhnmd->bhncm", queries, key_rows, precision=highest) * spread
    fading = queries * jnp.exp(levels)[..., None]
    final_level = levels[..., -1:]
    carried = key_rows * jnp.exp(final_level - levels)[..., None]

    def advance(memory, pieces):
        fading_part, keys_part, values_part, scores_part, carried_part, final_part = pieces
        update = values_part - jnp.einsum("bhcd,bhde->bhce", keys_part, memory, precision=highest)
        output = jnp.einsum("bhcd,bhde->bhce", fading_part, memory, precision=highest) + jnp.einsum(
            "bhcm,bhme->bhce", scores_part, update, precision=highest
        )
        memory = memory * jnp.exp(final_part)[..., None] + jnp.einsum(
            "bhcd,bhce->bhde", carried_part, update, precision=highest
        )
        return (memory, output)

    pieces = tuple(
        (
            jnp.moveaxis(array, 2, 0)
            for array in (fading, solved_keys, solved_values, scores, carried, final_level)
        )
    )
    initial = jnp.zeros((batch_size, head_count, key_dim, value_dim), queries.dtype)
    _, outputs = lax.scan(advance, initial, pieces)
    return jnp.moveaxis(outputs, 0, 2).reshape(batch_size, head_count, length, value_dim)


def token_mixer(projected, rate_logits, kernel, head_params, out_gain, segment):
    batch_size, length, _ = projected.shape
    head_count = head_params.shape[1]
    value_dim = out_gain.shape[0]
    channels = kernel.shape[1]
    key_width = (channels - head_count * value_dim) // 2
    key_dim = key_width // head_count
    mixed = short_conv(projected[..., :channels], kernel, segment)

    def heads_of(array, size):
        return jnp.moveaxis(array.reshape(batch_size, length, head_count, size), 2, 1)

    queries = heads_of(mixed[..., :key_width], key_dim)
    key_rows = heads_of(mixed[..., key_width : 2 * key_width], key_dim)
    value_rows = heads_of(mixed[..., 2 * key_width :], value_dim)
    queries = (
        queries
        * lax.rsqrt(jnp.sum(queries * queries, -1, keepdims=True) + 1e-06)
        * key_dim ** (-0.5)
    )
    key_rows = key_rows * lax.rsqrt(jnp.sum(key_rows * key_rows, -1, keepdims=True) + 1e-06)
    beta_gate = jax.nn.sigmoid(jnp.moveaxis(rate_logits[..., head_count:], 2, 1))
    decays = -jnp.exp(head_params[0])[:, None] * jax.nn.softplus(
        jnp.moveaxis(rate_logits[..., :head_count], 2, 1) + head_params[1][:, None]
    )
    earlier = jnp.pad(segment, ((0, 0), (1, 0)), constant_values=-1)[:, :length]
    decays = jnp.where((earlier != segment)[:, None, :], reset_level, decays)
    output = delta_rule(queries, key_rows, value_rows, beta_gate, decays, SPAN)
    output = output * lax.rsqrt(jnp.mean(output * output, -1, keepdims=True) + 1e-05) * out_gain
    gating = heads_of(projected[..., channels:], value_dim)
    return jnp.moveaxis(output * jax.nn.silu(gating), 1, 2).reshape(
        batch_size, length, head_count * value_dim
    )


def last_contract(left, right):
    return lax.dot_general(
        left, right, (((2,), (1,)), ((), ())), preferred_element_type=jnp.float32
    )


def layer_forward(entering, segment, weights, small_params):
    norm_gains, proj_weight, rate_weight, out_weight, up_weight, down_weight = weights
    kernel, head_params, out_gain = small_params
    widened = entering.astype(jnp.float32)
    normed_one, norm_one_back = jax.vjp(rms_gain, widened, norm_gains[0].astype(jnp.float32))
    hidden_one = normed_one.astype(jnp.bfloat16)
    projected = jnp.dot(hidden_one, proj_weight, preferred_element_type=jnp.float32)
    rate_logits = jnp.dot(hidden_one, rate_weight, preferred_element_type=jnp.float32)
    mixed_out, mixer_back = jax.vjp(
        partial(token_mixer, segment=segment), projected, rate_logits, kernel, head_params, out_gain
    )
    mixed_half = mixed_out.astype(jnp.bfloat16)
    stream = widened + last_contract(mixed_half, out_weight)
    normed_two, norm_two_back = jax.vjp(rms_gain, stream, norm_gains[1].astype(jnp.float32))
    hidden_two = normed_two.astype(jnp.bfloat16)
    gate_up = jnp.dot(hidden_two, up_weight, preferred_element_type=jnp.float32)
    activated, act_back = jax.vjp(swiglu, gate_up)
    act_half = activated.astype(jnp.bfloat16)
    layer_out = (stream + last_contract(act_half, down_weight)).astype(jnp.bfloat16)
    residuals = (
        norm_one_back,
        hidden_one,
        mixer_back,
        mixed_half,
        norm_two_back,
        hidden_two,
        act_back,
        act_half,
    )
    return (layer_out, residuals)


def layer_backward(cotangent_in, residuals, weights):
    norm_gains, proj_weight, rate_weight, out_weight, up_weight, down_weight = weights
    (
        norm_one_back,
        hidden_one,
        mixer_back,
        mixed_half,
        norm_two_back,
        hidden_two,
        act_back,
        act_half,
    ) = residuals
    dout_half = cotangent_in.astype(jnp.bfloat16)
    (gate_up_grad,) = act_back(jnp.dot(dout_half, down_weight, preferred_element_type=jnp.float32))
    gate_up_cot = gate_up_grad.astype(jnp.bfloat16)
    stream_grad, gain_two = norm_two_back(last_contract(gate_up_cot, up_weight))
    stream_grad = cotangent_in + stream_grad
    branch_cot = stream_grad.astype(jnp.bfloat16)
    proj_grad, rate_grad, kernel_grad, head_grad, out_gain_grad = mixer_back(
        jnp.dot(branch_cot, out_weight, preferred_element_type=jnp.float32)
    )
    proj_cot = proj_grad.astype(jnp.bfloat16)
    rate_cot = rate_grad.astype(jnp.bfloat16)
    hidden_grad = last_contract(proj_cot, proj_weight) + last_contract(rate_cot, rate_weight)
    entry_grad, gain_one = norm_one_back(hidden_grad)
    pairs = (
        hidden_one,
        proj_cot,
        rate_cot,
        mixed_half,
        branch_cot,
        hidden_two,
        gate_up_cot,
        act_half,
        dout_half,
    )
    return (
        stream_grad + entry_grad,
        pairs,
        (kernel_grad, head_grad, out_gain_grad),
        jnp.stack([gain_one, gain_two]),
    )


def weight_terms(pairs, gain_sum, start, count):
    flattened = [member.reshape(-1, member.shape[-1]) for member in pairs]
    (
        hidden_one,
        proj_cot,
        rate_cot,
        mixed_half,
        branch_cot,
        hidden_two,
        gate_up_cot,
        act_half,
        dout_half,
    ) = flattened

    def product(left, right):
        return lax.dot_general(
            left, right, (((0,), (0,)), ((), ())), preferred_element_type=jnp.float32
        )

    return jnp.concatenate(
        [
            product(hidden_one, proj_cot),
            product(hidden_one, rate_cot),
            product(branch_cot, mixed_half),
            product(hidden_two, gate_up_cot),
            product(dout_half, act_half),
            gain_sum.T,
        ],
        1,
    )


def split_term(total, widths):
    pieces = []
    column = 0
    for width in widths:
        pieces.append(total[..., column : column + width])
        column = column + width
    return pieces


def pass_forward(layer_out):
    return passed_along(layer_out, "section", 1)


def pass_backward(entry_grad):
    return passed_along(entry_grad.astype(jnp.bfloat16), "section", -1).astype(entry_grad.dtype)


def shards(
    tokens,
    segments,
    cotangent,
    norm_gains,
    proj_weight,
    rate_weight,
    out_weight,
    up_weight,
    down_weight,
    conv_kernels,
    head_params,
    out_gain,
):
    first_section = lax.axis_index("section") == 0
    weights = (
        lax.all_gather(norm_gains[0], "fsdp", axis=1, tiled=True),
        lax.all_gather(proj_weight[0], "fsdp", axis=0, tiled=True),
        lax.all_gather(rate_weight[0], "fsdp", axis=0, tiled=True),
        lax.all_gather(out_weight[0], "fsdp", axis=0, tiled=True),
        lax.all_gather(up_weight[0], "fsdp", axis=0, tiled=True),
        lax.all_gather(down_weight[0], "fsdp", axis=0, tiled=True),
    )
    small_params = (conv_kernels[0], head_params[0], out_gain[0])
    batches = tokens.shape[0]
    records = []
    results = []
    for forward_step in range(batches + 1):
        ahead_batch = min(forward_step, batches - 1)
        behind = max(forward_step - 1, 0)
        segment = jnp.where(first_section, segments[ahead_batch], segments[behind])
        if forward_step == 0:
            entering = tokens[0]
        else:
            entering = jnp.where(first_section, tokens[ahead_batch], pass_forward(results[-1]))
        produced, residuals = layer_forward(entering, segment, weights, small_params)
        records.append(residuals)
        results.append(produced)
    incoming = []
    kept_pairs = []
    small_list = []
    gain_list = []
    for backward_step in range(batches + 1):
        if backward_step < batches:
            own_cot = cotangent[batches - 1 - backward_step]
        else:
            own_cot = jnp.zeros_like(cotangent[0])
        if backward_step == 0:
            upstream = jnp.zeros_like(own_cot)
        else:
            upstream = pass_backward(incoming[-1])
        dout_full = jnp.where(first_section, upstream, own_cot)
        entry_grad, pairs, small_grads, gains_step = layer_backward(
            dout_full, records[batches - backward_step], weights
        )
        incoming.append(entry_grad)
        kept_pairs.append(pairs)
        small_list.append(small_grads)
        gain_list.append(gains_step)
    pairs_all = tuple((jnp.concatenate([member[i] for member in kept_pairs], 1) for i in range(9)))
    gain_sum = sum(gain_list)
    small_sum = tuple((sum((member[i] for member in small_list)) for i in range(3)))
    section_output = jnp.stack([jnp.where(first_section, results[0], results[1])])[None]
    input_grad = jnp.stack([jnp.where(first_section, incoming[batches], incoming[batches - 1])])[
        None
    ]
    own_rows = proj_weight.shape[1]
    term_of = partial(weight_terms, pairs_all, gain_sum)
    totals = lax.psum_scatter(
        term_of(jnp.int32(0), own_rows * lax.axis_size("fsdp")).astype(jnp.bfloat16),
        "fsdp",
        scatter_dimension=0,
        tiled=True,
    ).astype(jnp.float32)
    totals = lax.psum(totals.astype(jnp.bfloat16), "dp").astype(jnp.float32)
    kernel_grad, head_grad, out_gain_grad = lax.psum(
        (small_sum[0], small_sum[1], small_sum[2]), ("fsdp", "dp")
    )
    widths = [
        proj_weight.shape[2],
        rate_weight.shape[2],
        out_weight.shape[2],
        up_weight.shape[2],
        down_weight.shape[2],
        2,
    ]
    pieces = split_term(totals, widths)
    return (
        section_output,
        input_grad,
        pieces[5].T[None],
        pieces[0][None],
        pieces[1][None],
        pieces[2][None],
        pieces[3][None],
        pieces[4][None],
        kernel_grad[None],
        head_grad[None],
        out_gain_grad[None],
    )


def solution(mesh):
    return jax.shard_map(
        shards,
        mesh=mesh,
        in_specs=(
            P(None, ("fsdp", "dp"), None, None),
            P(None, ("fsdp", "dp"), None),
            P(None, ("fsdp", "dp"), None, None),
            P("section", None, "fsdp"),
            P("section", "fsdp", None),
            P("section", "fsdp", None),
            P("section", "fsdp", None),
            P("section", "fsdp", None),
            P("section", "fsdp", None),
            P("section", None, None),
            P("section", None, None),
            P("section", None),
        ),
        out_specs=(
            P("section", None, ("fsdp", "dp"), None, None),
            P("section", None, ("fsdp", "dp"), None, None),
            P("section", None, "fsdp"),
            P("section", "fsdp", None),
            P("section", "fsdp", None),
            P("section", "fsdp", None),
            P("section", "fsdp", None),
            P("section", "fsdp", None),
            P("section", None, None),
            P("section", None, None),
            P("section", None),
        ),
        check_vma=False,
    )
```

profile of v0, /device:TPU:0, one launch (start us, length us, event | category | flops | bytes accessed | tf_op | source)
XLA Modules:
  0.0 1455.5 jit_solution(11192671535240137623)
XLA Ops:
  10.3 12.7 all-gather
  23.2 13.7 all-gather.1
  41.3 86.5 %all-gather.11.cloned.1.call-done = bf16[1,1024,3072]{2,1,0:T(8,128)(2,1)} async-done(((bf16[1,256,3072]{2,1,0:T(8,128)(2,1)}), bf16[1,1024,3072]{2,1,0:T(8,128)(2,1)}) %all-gather.11.cloned.1.call-update) | async-done | bytes 6291472 | tf_op jit(solution)/shard_map/all_gather | solution.py:280
  141.4 39.3 %custom-call.16 = f32[1,4,2,1,64,64]{4,5,3,2,1,0:T(8,128)S(1)} custom-call(f32[1,4,2,1,64,64]{5,4,3,2,1,0:T(8,128)S(1)} %fusion.409), custom_call_target="InvertDiagBlocksLowerTriangular" | custom-call | tf_op jit(solution)/shard_map/jvp()/triangular_solve/custom-call.1 | solution.py:65
  185.2 7.1 while.96
  201.8 173.0 %all-gather.15.cloned.1.call-done = bf16[1,1024,5632]{2,1,0:T(8,128)(2,1)} async-done(((bf16[1,256,5632]{2,1,0:T(8,128)(2,1)}), bf16[1,1024,5632]{2,1,0:T(8,128)(2,1)}) %all-gather.15.cloned.1.call-update) | async-done | bytes 11534352 | tf_op jit(solution)/shard_map/all_gather | solution.py:283
  374.8 6.0 fusion.166
  382.8 98.3 %all-gather.17.cloned.1.call-done = bf16[1,1024,2816]{2,1,0:T(8,128)(2,1)} async-done(((bf16[1,256,2816]{2,1,0:T(8,128)(2,1)}), bf16[1,1024,2816]{2,1,0:T(8,128)(2,1)}) %all-gather.17.cloned.1.call-update) | async-done | bytes 5767184 | tf_op jit(solution)/shard_map/all_gather | solution.py:284
  481.2 4.6 fusion.242
  515.8 40.7 %custom-call.17 = f32[1,4,2,1,64,64]{4,5,3,2,1,0:T(8,128)} custom-call(f32[1,4,2,1,64,64]{5,4,3,2,1,0:T(8,128)} %fusion.397), custom_call_target="InvertDiagBlocksLowerTriangular" | custom-call | tf_op jit(solution)/shard_map/jvp()/triangular_solve/custom-call.1 | solution.py:65
  576.0 11.5 while.97
  599.8 6.1 fusion.169
  622.0 26.4 %while.98 = (s32[]{:T(128)}, f32[1,4,128,256]{2,3,1,0:T(8,128)S(1)}, f32[2,1,4,64,128]{4,3,0,2,1:T(8,128)}, f32[2,1,4,64,128]{4,3,2,1,0:T(8,128)}, f32[2,1,4,64,...) while((s32[]{:T(128)}, ...), condition=%wide.region_20.23_spmd.clone, body=%wide.region_18.22_spmd.clone.sunk | while | flops 706019328 | bytes 25702096 | solution.py:93
  702.5 4.9 fusion.436
  720.8 19.1 %while.99 = (s32[]{:T(128)}, f32[1,4,128,256]{2,3,1,0:T(8,128)S(1)}, f32[2,1,4,64,128]{4,3,0,2,1:T(8,128)}, f32[2,1,4,64,128]{4,3,2,1,0:T(8,128)}, f32[2,1,4,64,...) while((s32[]{:T(128)}, ...), condition=%wide.region_37.42_spmd.clone, body=%wide.region_35.41_spmd.clone.sunk | while | flops 706019328 | bytes 25701472 | solution.py:93
  762.4 5.6 multiply_reduce_fusion.3
  785.2 4.5 convolution_convert_fusion.2
  796.2 7.3 convolution_convert_fusion
  803.8 5.7 convolution_convert_fusion.1
  809.5 48.0 %concatenate.48 = bf16[1024,12554]{1,0:T(8,128)(2,1)} concatenate(bf16[1024,3072]{1,0:T(8,128)(2,1)} %convolution_convert_fusion.2, bf16[1024,8]{1,0:T(8,128)(2,1)S(1)} %copy.593, bf16[1024,1024]{1,0:T(8,128)(2,1)S(1)} %copy-done.42, bf16[1024,5632]{1,0:T(8,128)(2,1)} %convolution_convert_fusion, bf16[1024,2816]{1,0:T(8,128)(2,1)} %convolution_convert_fusion.1, ...), dimensions={1} | concatenate | bytes 51421184 | tf_op jit(solution)/shard_map/concatenate | solution.py:233
  857.5 427.1 %reduce-scatter.2.cloned.1.call-done = bf16[256,12554]{1,0:T(8,128)(2,1)} async-done(((bf16[1024,12554]{1,0:T(8,128)(2,1)}), bf16[256,12554]{1,0:T(8,128)(2,1)}) %reduce-scatter.2.cloned.1.call-update) | async-done | bytes 6427664 | tf_op jit(solution)/shard_map/reduce_scatter | solution.py:331
  1285.9 5.3 fusion.264
  1291.4 79.9 %all-reduce.51 = (f32[1,4,2048]{2,1,0:T(4,128)}, f32[1,2,4]{2,1,0:T(2,128)}, f32[1,256]{1,0:T(1,128)}) all-reduce(f32[1,4,2048]{2,1,0:T(4,128)S(1)} %add_bitcast_fusion.2, f32[1,2,4]{2,1,0:T(2,128)S(1)} %add_bitcast_fusion.3, f32[1,256]{1,0:T(1,128)S(1)} %bitcast.1621), channel_id=1, replica_groups=mesh['section'=2,'fsdp'=4,'dp'=4] {'fsdp','dp'}, use_global_device_ids=true, to_apply=%region_64.69 | all-reduce | flops 8456 | bytes 67648 | tf_op jit(solution)/shard_map/psum | solution.py:338
  1371.3 62.2 %all-reduce.54.cloned.1.call-done = bf16[256,12554]{1,0:T(8,128)(2,1)} async-done(((bf16[256,12554]{1,0:T(8,128)(2,1)}), bf16[256,12554]{1,0:T(8,128)(2,1)}) %all-reduce.54.cloned.1.call-update) | async-done | bytes 6427664 | tf_op jit(solution)/shard_map/psum | solution.py:337
  (1054 shorter events, 303.8 us)
Async XLA Ops:
  7.2 120.7 %all-gather.11.cloned.1.call-start = ((), (), s32[]{:S(2)}) async-start(), calls=%async_computation.3 | async-start | bytes 7864320 | tf_op jit(solution)/shard_map/all_gather | solution.py:280
  7.9 191.2 %all-gather.13.cloned.1.call-start = ((), (), s32[]{:S(2)}) async-start(), calls=%async_computation.4 | async-start | bytes 2621440 | tf_op jit(solution)/shard_map/all_gather | solution.py:282
  8.7 366.1 %all-gather.15.cloned.1.call-start = ((), (), s32[]{:S(2)}) async-start(), calls=%async_computation.5 | async-start | bytes 14417920 | tf_op jit(solution)/shard_map/all_gather | solution.py:283
  9.5 471.7 %all-gather.17.cloned.1.call-start = ((), (), s32[]{:S(2)}) async-start(), calls=%async_computation.6 | async-start | bytes 7208960 | tf_op jit(solution)/shard_map/all_gather | solution.py:284
  10.0 1274.6 %reduce-scatter.2.cloned.1.call-start = ((), (), s32[]{:S(2)}) async-start(), calls=%async_computation.1 | async-start | bytes 32440320 | tf_op jit(solution)/shard_map/reduce_scatter | solution.py:331
  10.1 130.4 %copy-start.154 = (f32[64,64]{1,0:T(8,128)}, f32[64,64]{1,0:T(8,128)S(1)}, u32[]{:S(2)}) copy-start(f32[64,64]{1,0:T(8,128)S(1)} %get-tuple-element.1668) | copy-start | bytes 49156
  10.1 130.4 %copy-start.161 = (pred[64,64]{1,0:T(8,128)(4,1)}, pred[64,64]{1,0:T(8,128)(4,1)S(1)}, u32[]{:S(2)}) copy-start(pred[64,64]{1,0:T(8,128)(4,1)S(1)} %get-tuple-element.1667) | copy-start | bytes 12292
  10.3 121.5 %copy-start.198 = (pred[128]{0:T(512)(128)(4,1)}, pred[128]{0:T(512)(128)(4,1)S(1)}, u32[]{:S(2)}) copy-start(pred[128]{0:T(512)(128)(4,1)S(1)} %get-tuple-element.1642) | copy-start | bytes 388
  10.3 121.5 %copy-start.202 = (pred[128]{0:T(512)(128)(4,1)}, pred[128]{0:T(512)(128)(4,1)S(1)}, u32[]{:S(2)}) copy-start(pred[128]{0:T(512)(128)(4,1)S(1)} %get-tuple-element.1646) | copy-start | bytes 388
  10.3 121.5 %copy-start.206 = (pred[128]{0:T(512)(128)(4,1)}, pred[128]{0:T(512)(128)(4,1)S(1)}, u32[]{:S(2)}) copy-start(pred[128]{0:T(512)(128)(4,1)S(1)} %get-tuple-element.1647) | copy-start | bytes 388
  23.0 351.8 %copy-start.151 = (f32[1,1,1024]{2,1,0:T(1,128)}, f32[1,1,1024]{2,1,0:T(1,128)S(1)}, u32[]{:S(2)}) copy-start(f32[1,1,1024]{2,1,0:T(1,128)S(1)} %get-tuple-element.1629) | copy-start | bytes 12292
  23.0 468.9 %copy-start.149 = (f32[1,1,1024]{2,1,0:T(1,128)}, f32[1,1,1024]{2,1,0:T(1,128)S(1)}, u32[]{:S(2)}) copy-start(f32[1,1,1024]{2,1,0:T(1,128)S(1)} %get-tuple-element.1630) | copy-start | bytes 12292
  23.2 108.5 %copy-start.239 = (f32[128]{0:T(128)}, f32[128]{0:T(128)S(1)}, u32[]{:S(2)}) copy-start(f32[128]{0:T(128)S(1)} %fusion.515) | copy-start | bytes 1540
  36.9 455.1 %copy-start.159 = (bf16[1,1024,8]{1,2,0:T(8,128)(2,1)}, bf16[1,1024,8]{1,2,0:T(8,128)(2,1)S(1)}, u32[]{:S(2)}) copy-start(bf16[1,1024,8]{1,2,0:T(8,128)(2,1)S(1)} %all-gather.1) | copy-start | bytes 49156
  40.5 97.1 %copy-start.177 = (f32[4,2,64]{2,1,0:T(2,128)}, f32[4,2,64]{2,1,0:T(2,128)S(1)}, u32[]{:S(2)}) copy-start(f32[4,2,64]{2,1,0:T(2,128)S(1)} %get-tuple-element.1632) | copy-start | bytes 6148
  40.5 97.1 %copy-start.181 = (f32[4,2,64]{2,1,0:T(2,128)}, f32[4,2,64]{2,1,0:T(2,128)S(1)}, u32[]{:S(2)}) copy-start(f32[4,2,64]{2,1,0:T(2,128)S(1)} %get-tuple-element.1633) | copy-start | bytes 6148
  40.6 140.2 %copy-start.155 = (f32[4,2,64]{2,1,0:T(2,128)}, f32[4,2,64]{2,1,0:T(2,128)S(1)}, u32[]{:S(2)}) copy-start(f32[4,2,64]{2,1,0:T(2,128)S(1)} %mul.1564) | copy-start | bytes 6148
  201.8 179.1 %copy-start.275 = (f32[128]{0:T(128)}, f32[128]{0:T(128)S(1)}, u32[]{:S(2)}) copy-start(f32[128]{0:T(128)S(1)} %get-tuple-element.1648) | copy-start | bytes 1540
  201.8 279.4 %copy-start.2 = (f32[128,1024]{1,0:T(8,128)}, f32[128,1024]{1,0:T(8,128)S(1)}, u32[]{:S(2)}) copy-start(f32[128,1024]{1,0:T(8,128)S(1)} %get-tuple-element.1649) | copy-start | bytes 1572868
  201.8 179.0 %copy-start.241 = (f32[128]{0:T(128)}, f32[128]{0:T(128)S(1)}, u32[]{:S(2)}) copy-start(f32[128]{0:T(128)S(1)} %fusion.516) | copy-start | bytes 1540
  382.8 103.0 %copy-start.68 = (bf16[1,128,2816]{2,1,0:T(8,128)(2,1)}, bf16[1,128,2816]{2,1,0:T(8,128)(2,1)S(1)}, u32[]{:S(2)}) copy-start(bf16[1,128,2816]{2,1,0:T(8,128)(2,1)S(1)} %multiply_convert_fusion.1) | copy-start | bytes 2162692
  485.8 5.9 collective-permute-start
  697.8 4.6 collective-permute-start.1
  857.5 576.0 %all-reduce.54.cloned.1.call-start = ((), (), s32[]{:S(2)}) async-start(), calls=%async_computation.2 | async-start | bytes 12976128 | tf_op jit(solution)/shard_map/psum | solution.py:337
  (320 other events, 1955.4 us)
Sparse Core Ops, SparseCore 0:
  9.6 118.2 all-gather.10
  129.4 44.0 all-gather.12
  175.1 199.6 all-gather.14
  376.2 104.9 all-gather.16
  857.6 426.9 reduce-scatter.1
  1287.8 145.6 all-reduce.53
where the time goes:
time: 1470 us; the launch traced here: 1460 us
  waiting for transfers between devices  850 us (58%)
  other arithmetic  163 us (11%)
  local copies, waits for them, and re-layouts  161 us (11%)
  matrix products  151 us (10%)
  blocking collectives  106 us (7%)
  between operations  17.9 us (1%)
    reduce_scatter x1, waiting for transfers between devices, shards(): lax.psum_scatter(term_of(jnp.int32(0), own_rows * lax.axis_size('fsdp'))....  427 us
    all_gather x1, waiting for transfers between devices, shards(): lax.all_gather(up_weight[0], 'fsdp', axis=0, tiled=True)  173 us
    all_gather x1, waiting for transfers between devices, shards(): lax.all_gather(down_weight[0], 'fsdp', axis=0, tiled=True)  98.3 us
    all_gather x1, waiting for transfers between devices, shards(): lax.all_gather(proj_weight[0], 'fsdp', axis=0, tiled=True)  86.5 us
    another operation x6, other arithmetic, delta_rule(): lax.linalg.triangular_solve(system, right_side, left_side=True, lower=Tru...  83.3 us
    psum x1, blocking collectives, shards(): lax.psum((small_sum[0], small_sum[1], small_sum[2]), ('fsdp', 'dp'))  79.9 us
    psum x1, waiting for transfers between devices, shards(): totals = lax.psum(totals.astype(jnp.bfloat16), 'dp').astype(jnp.float32)  62.2 us
    concatenate x1, local copies, waits for them, and re-layouts, weight_terms(): jnp.concatenate([product(hidden_one, proj_cot), product(hidden_one, rate_...  48 us
  transfers between devices with their start and end apart: 8, of which 5 were waited for; matrix products, arithmetic and copies ran while one was open for 6% of the time, Pallas kernels for 0%

commit v1 on v0

--- a/solution.py
+++ b/solution.py
@@ -1,3 +1,4 @@
+import functools
 from functools import partial
 import jax
 import jax.numpy as jnp
@@ -7,6 +8,36 @@
 SPAN = 64
 highest = lax.Precision.HIGHEST
 reset_level = -30.0
+
+
+def replace_body_in(target, a_name):
+    z1 = lax.axis_size(a_name)
+    taken_in = lax.axis_index(a_name)
+    p_next, shaped, fresh = (z1, taken_in, target.shape[0])
+    blocks_here = []
+    for dev_i in range(p_next):
+        blocks_here.append((dev_i, (dev_i + 1) % p_next))
+    parts_seen = []
+    for dev_i in range(p_next):
+        parts_seen.append((dev_i, (dev_i - 1) % p_next))
+    frame_out = jnp.zeros((*target.shape[:0], p_next * fresh, *target.shape[1:]), target.dtype)
+    frame_out = lax.dynamic_update_slice_in_dim(frame_out, target, shaped * fresh, axis=0)
+    f_now = p_next // 2
+    latest = left_arr = target
+    for dd in range(1, f_now + 1):
+        latest = lax.ppermute(latest, axis_name=a_name, perm=blocks_here)
+        frame_out = lax.dynamic_update_slice_in_dim(
+            frame_out, latest, (shaped - dd) % p_next * fresh, axis=0
+        )
+        if dd < p_next - f_now:
+            left_arr = lax.ppermute(left_arr, a_name, parts_seen)
+            frame_out = lax.dynamic_update_slice_in_dim(
+                frame_out, left_arr, (shaped + dd) % p_next * fresh, axis=0
+            )
+    return frame_out
+
+
+_change_goods = functools.partial(replace_body_in, a_name="fsdp")
 
 
 def passed_along(value, axis, steps):
@@ -277,7 +308,7 @@
     first_section = lax.axis_index("section") == 0
     weights = (
         lax.all_gather(norm_gains[0], "fsdp", axis=1, tiled=True),
-        lax.all_gather(proj_weight[0], "fsdp", axis=0, tiled=True),
+        _change_goods(proj_weight[0]),
         lax.all_gather(rate_weight[0], "fsdp", axis=0, tiled=True),
         lax.all_gather(out_weight[0], "fsdp", axis=0, tiled=True),
         lax.all_gather(up_weight[0], "fsdp", axis=0, tiled=True),

time: 1470 us -> 1410 us (0.959)
  waiting for transfers between devices: 850 us -> 691 us
  blocking collectives: 106 us -> 216 us
    all_gather x1, waiting for transfers between devices: 173 us -> 36.2 us  [shards(): lax.all_gather(up_weight[0], 'fsdp', axis=0, tiled=True)]
    all_gather x1, blocking collectives: 12.7 us -> 109 us  [shards(): lax.all_gather(norm_gains[0], 'fsdp', axis=1, tiled=True)]
    all_gather x1 -> x0, waiting for transfers between devices: 86.5 us -> none  [shards(): lax.all_gather(proj_weight[0], 'fsdp', axis=0, tiled=True)]
    ppermute x0 -> x3, waiting for transfers between devices: none -> 65 us  [the longest x2 65 us: replace_body_in(): latest = lax.ppermute(latest, axis_name=a_name, perm=blocks_here)]
  transfers between devices with their start and end apart: 8 -> 10, of which waited for: 5 -> 5; matrix products, arithmetic and copies ran while one was open for 6% -> 7% of each run, Pallas kernels for 0% -> 0%
where the time goes in v1:
time: 1410 us; the launch traced here: 1400 us
  waiting for transfers between devices  691 us (49%)
  blocking collectives  216 us (15%)
  local copies, waits for them, and re-layouts  167 us (12%)
  other arithmetic  151 us (11%)
  matrix products  149 us (11%)
  between operations  17.5 us (1%)
    reduce_scatter x1, waiting for transfers between devices, shards(): lax.psum_scatter(term_of(jnp.int32(0), own_rows * lax.axis_size('fsdp'))....  427 us
    all_gather x1, blocking collectives, shards(): lax.all_gather(norm_gains[0], 'fsdp', axis=1, tiled=True)  109 us
    all_gather x1, waiting for transfers between devices, shards(): lax.all_gather(down_weight[0], 'fsdp', axis=0, tiled=True)  99.4 us
    another operation x6, other arithmetic, delta_rule(): lax.linalg.triangular_solve(system, right_side, left_side=True, lower=Tru...  83.2 us
    psum x1, blocking collectives, shards(): lax.psum((small_sum[0], small_sum[1], small_sum[2]), ('fsdp', 'dp'))  79.6 us
    ppermute x2, waiting for transfers between devices, replace_body_in(): latest = lax.ppermute(latest, axis_name=a_name, perm=blocks_here)  65 us
    psum x1, waiting for transfers between devices, shards(): totals = lax.psum(totals.astype(jnp.bfloat16), 'dp').astype(jnp.float32)  62.4 us
    concatenate x1, local copies, waits for them, and re-layouts, weight_terms(): jnp.concatenate([product(hidden_one, proj_cot), product(hidden_one, rate_...  47.9 us
  transfers between devices with their start and end apart: 10, of which 5 were waited for; matrix products, arithmetic and copies ran while one was open for 7% of the time, Pallas kernels for 0%

profile of v1, /device:TPU:0, one launch (start us, length us, event | category | flops | bytes accessed | tf_op | source)
XLA Modules:
  0.0 1403.8 jit_solution(12241585020248413162)
XLA Ops:
  14.3 109.1 %all-gather = bf16[1,2,1024]{2,1,0:T(2,128)(2,1)S(1)} all-gather(bf16[1,2,256]{2,1,0:T(2,128)(2,1)S(1)} %copy-done.258), channel_id=2, replica_groups=mesh['section'=2,'fsdp'=4,'dp'=4] {'fsdp'}, dimensions={2}, use_global_device_ids=true | all-gather | bytes 5120 | tf_op jit(solution)/shard_map/all_gather | solution.py:310
  123.6 27.2 %all-gather.1 = bf16[1,1024,8]{1,2,0:T(8,128)(2,1)S(1)} all-gather(bf16[1,256,8]{1,2,0:T(8,128)(2,1)S(1)} %copy-done.247), channel_id=3, replica_groups=mesh['section'=2,'fsdp'=4,'dp'=4] {'fsdp'}, dimensions={1}, use_global_device_ids=true | all-gather | bytes 20480 | tf_op jit(solution)/shard_map/all_gather | solution.py:312
  160.7 65.0 %collective-permute-done.2 = bf16[256,3072]{1,0:T(8,128)(2,1)S(1)} collective-permute-done((bf16[256,3072]{1,0:T(8,128)(2,1)}, bf16[256,3072]{1,0:T(8,128)(2,1)S(1)}, u32[]{:S(2)}, u32[]{:S(2)}) %collective-permute-start.2) | collective-permute-done | bytes 1572896 | tf_op jit(solution)/shard_map/ppermute | solution.py:28
  239.1 39.9 %custom-call.16 = f32[1,4,2,1,64,64]{4,5,3,2,1,0:T(8,128)S(1)} custom-call(f32[1,4,2,1,64,64]{5,4,3,2,1,0:T(8,128)S(1)} %fusion.395), custom_call_target="InvertDiagBlocksLowerTriangular" | custom-call | tf_op jit(solution)/shard_map/jvp()/triangular_solve/custom-call.1 | solution.py:96
  283.4 6.8 while.96
  299.8 36.2 %all-gather.11.cloned.1.call-done = bf16[1,1024,5632]{2,1,0:T(8,128)(2,1)} async-done(((bf16[1,256,5632]{2,1,0:T(8,128)(2,1)}), bf16[1,1024,5632]{2,1,0:T(8,128)(2,1)}) %all-gather.11.cloned.1.call-update) | async-done | bytes 11534352 | tf_op jit(solution)/shard_map/all_gather | solution.py:314
  336.0 6.0 fusion.166
  344.0 99.4 %all-gather.13.cloned.1.call-done = bf16[1,1024,2816]{2,1,0:T(8,128)(2,1)} async-done(((bf16[1,256,2816]{2,1,0:T(8,128)(2,1)}), bf16[1,1024,2816]{2,1,0:T(8,128)(2,1)}) %all-gather.13.cloned.1.call-update) | async-done | bytes 5767184 | tf_op jit(solution)/shard_map/all_gather | solution.py:315
  443.4 4.6 fusion.228
  478.0 40.7 %custom-call.17 = f32[1,4,2,1,64,64]{4,5,3,2,1,0:T(8,128)} custom-call(f32[1,4,2,1,64,64]{5,4,3,2,1,0:T(8,128)} %fusion.383), custom_call_target="InvertDiagBlocksLowerTriangular" | custom-call | tf_op jit(solution)/shard_map/jvp()/triangular_solve/custom-call.1 | solution.py:96
  539.2 11.3 while.97
  562.8 6.1 fusion.169
  584.9 26.6 %while.98 = (s32[]{:T(128)}, f32[1,4,128,256]{2,3,1,0:T(8,128)S(1)}, f32[2,1,4,64,128]{4,3,0,2,1:T(8,128)}, f32[2,1,4,64,128]{4,3,2,1,0:T(8,128)}, f32[2,1,4,64,...) while((s32[]{:T(128)}, ...), condition=%wide.region_20.23_spmd.clone, body=%wide.region_18.22_spmd.clone.sunk | while | flops 706019328 | bytes 25702096 | solution.py:124
  656.6 4.9 fusion.422
  675.0 19.0 %while.99 = (s32[]{:T(128)}, f32[1,4,128,256]{2,3,1,0:T(8,128)S(1)}, f32[2,1,4,64,128]{4,3,0,2,1:T(8,128)}, f32[2,1,4,64,128]{4,3,2,1,0:T(8,128)}, f32[2,1,4,64,...) while((s32[]{:T(128)}, ...), condition=%wide.region_37.42_spmd.clone, body=%wide.region_35.41_spmd.clone.sunk | while | flops 706019328 | bytes 25701472 | solution.py:124
  721.5 5.3 multiply_reduce_fusion.3
  733.9 4.5 convolution_convert_fusion.2
  745.0 7.1 convolution_convert_fusion
  752.3 5.9 convolution_convert_fusion.1
  758.2 47.9 %concatenate.48 = bf16[1024,12554]{1,0:T(8,128)(2,1)} concatenate(bf16[1024,3072]{1,0:T(8,128)(2,1)} %convolution_convert_fusion.2, bf16[1024,8]{1,0:T(8,128)(2,1)S(1)} %copy.593, bf16[1024,1024]{1,0:T(8,128)(2,1)S(1)} %copy-done.42, bf16[1024,5632]{1,0:T(8,128)(2,1)} %convolution_convert_fusion, bf16[1024,2816]{1,0:T(8,128)(2,1)} %convolution_convert_fusion.1, ...), dimensions={1} | concatenate | bytes 51421184 | tf_op jit(solution)/shard_map/concatenate | solution.py:264
  806.2 427.1 %reduce-scatter.2.cloned.1.call-done = bf16[256,12554]{1,0:T(8,128)(2,1)} async-done(((bf16[1024,12554]{1,0:T(8,128)(2,1)}), bf16[256,12554]{1,0:T(8,128)(2,1)}) %reduce-scatter.2.cloned.1.call-update) | async-done | bytes 6427664 | tf_op jit(solution)/shard_map/reduce_scatter | solution.py:362
  1234.6 5.3 fusion.250
  1240.1 79.6 %all-reduce.51 = (f32[1,4,2048]{2,1,0:T(4,128)}, f32[1,2,4]{2,1,0:T(2,128)}, f32[1,256]{1,0:T(1,128)}) all-reduce(f32[1,4,2048]{2,1,0:T(4,128)S(1)} %add_bitcast_fusion.2, f32[1,2,4]{2,1,0:T(2,128)S(1)} %add_bitcast_fusion.3, f32[1,256]{1,0:T(1,128)S(1)} %bitcast.1610), channel_id=1, replica_groups=mesh['section'=2,'fsdp'=4,'dp'=4] {'fsdp','dp'}, use_global_device_ids=true, to_apply=%region_64.69 | all-reduce | flops 8456 | bytes 67648 | tf_op jit(solution)/shard_map/psum | solution.py:369
  1319.7 62.4 %all-reduce.54.cloned.1.call-done = bf16[256,12554]{1,0:T(8,128)(2,1)} async-done(((bf16[256,12554]{1,0:T(8,128)(2,1)}), bf16[256,12554]{1,0:T(8,128)(2,1)}) %all-reduce.54.cloned.1.call-update) | async-done | bytes 6427664 | tf_op jit(solution)/shard_map/psum | solution.py:368
  (1044 shorter events, 300.0 us)
Async XLA Ops:
  7.2 289.9 %all-gather.9.cloned.1.call-start = ((), (), s32[]{:S(2)}) async-start(), calls=%async_computation.3 | async-start | bytes 2621440 | tf_op jit(solution)/shard_map/all_gather | solution.py:313
  7.9 115.5 %copy-start.19 = (bf16[1,1,128,1024]{3,2,1,0:T(8,128)(2,1)S(1)}, bf16[1,1,128,1024]{3,2,1,0:T(8,128)(2,1)}, u32[]{:S(2)}) copy-start(bf16[1,1,128,1024]{3,2,1,0:T(8,128)(2,1)} %param.27) | copy-start | bytes 786436
  8.0 115.6 %copy-start.247 = (bf16[1,256,8]{1,2,0:T(8,128)(2,1)S(1)}, bf16[1,256,8]{1,2,0:T(8,128)(2,1)}, u32[]{:S(2)}) copy-start(bf16[1,256,8]{1,2,0:T(8,128)(2,1)} %param.32) | copy-start | bytes 12292
  8.0 145.8 %copy-start.188 = (f32[1,4,2048]{2,1,0:T(4,128)S(1)}, f32[1,4,2048]{2,1,0:T(4,128)}, u32[]{:S(2)}) copy-start(f32[1,4,2048]{2,1,0:T(4,128)} %param.36) | copy-start | bytes 98308
  8.0 328.0 %all-gather.11.cloned.1.call-start = ((), (), s32[]{:S(2)}) async-start(), calls=%async_computation.4 | async-start | bytes 14417920 | tf_op jit(solution)/shard_map/all_gather | solution.py:314
  8.7 434.7 %all-gather.13.cloned.1.call-start = ((), (), s32[]{:S(2)}) async-start(), calls=%async_computation.5 | async-start | bytes 7208960 | tf_op jit(solution)/shard_map/all_gather | solution.py:315
  8.8 145.2 %collective-permute-start = (bf16[256,3072]{1,0:T(8,128)(2,1)}, bf16[256,3072]{1,0:T(8,128)(2,1)}, u32[]{:S(2)}, u32[]{:S(2)}) collective-permute-start(bf16[256,3072]{1,0:T(8,128)(2,1)} %bitcast.12), channel_id=1, source_target_pairs={{0,4},{4,8},{8,12},{12,0},{1,5},{5,9},{9,13},{13,1},{2,6},{6,10},{... | collective-permute-start | bytes 4718600 | tf_op jit(solution)/shard_map/ppermute | solution.py:28
  11.9 147.3 %collective-permute-start.1 = (bf16[256,3072]{1,0:T(8,128)(2,1)}, bf16[256,3072]{1,0:T(8,128)(2,1)}, u32[]{:S(2)}, u32[]{:S(2)}) collective-permute-start(bf16[256,3072]{1,0:T(8,128)(2,1)} %bitcast.12), channel_id=1, source_target_pairs={{0,12},{4,0},{8,4},{12,8},{1,13},{5,1},{9,5},{13,9},{2,14},{6,2},{... | collective-permute-start | bytes 4718600 | tf_op jit(solution)/shard_map/ppermute | solution.py:33
  14.0 1219.3 %reduce-scatter.2.cloned.1.call-start = ((), (), s32[]{:S(2)}) async-start(), calls=%async_computation.1 | async-start | bytes 32440320 | tf_op jit(solution)/shard_map/reduce_scatter | solution.py:362
  14.1 137.1 %copy-start.222 = (f32[4]{0:T(128)}, f32[4]{0:T(128)S(1)}, u32[]{:S(2)}) copy-start(f32[4]{0:T(128)S(1)} %get-tuple-element.1644) | copy-start | bytes 52
  14.1 139.1 %copy-start.224 = (f32[4]{0:T(128)}, f32[4]{0:T(128)S(1)}, u32[]{:S(2)}) copy-start(f32[4]{0:T(128)S(1)} %get-tuple-element.1645) | copy-start | bytes 52
  14.2 139.0 %copy-start.226 = (pred[128]{0:T(512)(128)(4,1)}, pred[128]{0:T(512)(128)(4,1)S(1)}, u32[]{:S(2)}) copy-start(pred[128]{0:T(512)(128)(4,1)S(1)} %get-tuple-element.1643) | copy-start | bytes 388
  14.3 214.3 %copy-start.193 = (pred[128]{0:T(512)(128)(4,1)}, pred[128]{0:T(512)(128)(4,1)S(1)}, u32[]{:S(2)}) copy-start(pred[128]{0:T(512)(128)(4,1)S(1)} %get-tuple-element.1642) | copy-start | bytes 388
  14.3 214.3 %copy-start.197 = (pred[128]{0:T(512)(128)(4,1)}, pred[128]{0:T(512)(128)(4,1)S(1)}, u32[]{:S(2)}) copy-start(pred[128]{0:T(512)(128)(4,1)S(1)} %get-tuple-element.1646) | copy-start | bytes 388
  14.3 214.3 %copy-start.201 = (pred[128]{0:T(512)(128)(4,1)}, pred[128]{0:T(512)(128)(4,1)S(1)}, u32[]{:S(2)}) copy-start(pred[128]{0:T(512)(128)(4,1)S(1)} %get-tuple-element.1647) | copy-start | bytes 388
  123.4 212.6 %copy-start.151 = (f32[1,1,1024]{2,1,0:T(1,128)}, f32[1,1,1024]{2,1,0:T(1,128)S(1)}, u32[]{:S(2)}) copy-start(f32[1,1,1024]{2,1,0:T(1,128)S(1)} %get-tuple-element.1629) | copy-start | bytes 12292
  123.4 330.9 %copy-start.149 = (f32[1,1,1024]{2,1,0:T(1,128)}, f32[1,1,1024]{2,1,0:T(1,128)S(1)}, u32[]{:S(2)}) copy-start(f32[1,1,1024]{2,1,0:T(1,128)S(1)} %get-tuple-element.1630) | copy-start | bytes 12292
  150.8 303.6 %copy-start.159 = (bf16[1,1024,8]{1,2,0:T(8,128)(2,1)}, bf16[1,1024,8]{1,2,0:T(8,128)(2,1)S(1)}, u32[]{:S(2)}) copy-start(bf16[1,1024,8]{1,2,0:T(8,128)(2,1)S(1)} %all-gather.1) | copy-start | bytes 49156
  153.2 125.8 %copy-start.155 = (f32[4,2,64]{2,1,0:T(2,128)}, f32[4,2,64]{2,1,0:T(2,128)S(1)}, u32[]{:S(2)}) copy-start(f32[4,2,64]{2,1,0:T(2,128)S(1)} %mul.1580) | copy-start | bytes 6148
  154.0 71.7 %collective-permute-start.2 = (bf16[256,3072]{1,0:T(8,128)(2,1)}, bf16[256,3072]{1,0:T(8,128)(2,1)S(1)}, u32[]{:S(2)}, u32[]{:S(2)}) collective-permute-start(bf16[256,3072]{1,0:T(8,128)(2,1)} %collective-permute-done), channel_id=1, source_target_pairs={{0,4},{4,8},{8,12},{12,0},{1,5},{5,9},{9,13},{13,1},{2,6},{6,10},{... | collective-permute-start | bytes 4718600 | tf_op jit(solution)/shard_map/ppermute | solution.py:28
  299.8 143.7 %copy-start.3 = (f32[128,1024]{1,0:T(8,128)}, f32[128,1024]{1,0:T(8,128)S(1)}, u32[]{:S(2)}) copy-start(f32[128,1024]{1,0:T(8,128)S(1)} %get-tuple-element.1649) | copy-start | bytes 1572868
  448.0 6.0 collective-permute-start.3
  652.1 4.4 collective-permute-start.4
  806.2 576.0 %all-reduce.54.cloned.1.call-start = ((), (), s32[]{:S(2)}) async-start(), calls=%async_computation.2 | async-start | bytes 12976128 | tf_op jit(solution)/shard_map/psum | solution.py:368
  (313 other events, 2292.7 us)
Sparse Core Ops, SparseCore 0:
  9.6 89.9 all-gather.8
  101.1 234.8 all-gather.10
  337.6 105.8 all-gather.12
  806.3 426.9 reduce-scatter.1
  1236.5 145.6 all-reduce.53
